TPU v7x, 256 devices: a whole 4x4x8 slice. The times are simulated.
256 devices in a mesh: row: 8 (over x, y_lo), col: 32 (over z, y_hi, core).
Axes of the slice: x: 4, y: 4 (y_hi: 2, y_lo: 2; y = y_hi * 2 + y_lo), z: 8, core: 2. Of those that a mesh axis runs over, the one named last changes fastest.
Arguments:
- ancestor_inverse: float32 [16384, 16384], P('row', 'col'), may hold values from -6 to 6
- panel: float32 [6, 64, 256, 256], P(None, 'row', 'col'), may hold values from -0.0625 to 0.0625
- diag_inverse: float32 [6, 256, 256], replicated, as said below
- structure: int32 [6, 32], replicated, may hold values from 0 to 63, as said below
- block_slot: int32 [64], replicated, may hold values from 0 to 63, as said below
Outputs:
- off_block: float32 [6, 64, 256, 256], P(None, 'row', 'col')
- diag_block: float32 [6, 256, 256], replicated
Inputs may be any that keep to these rules, and one draw needn't show every extreme that they name: `structure`: the 32 entries of a supernode are distinct global row blocks. Mapped through block_slot, at most 6 of them fall into any aligned run of 8 storage slots, and for every supernode some run holds exactly 6. `block_slot`: A permutation of the 64 row blocks. `diag_inverse`: lower triangular with a positive diagonal.
All inputs are finite; a program needn't handle non-finite values.
Results may differ from a plain program's by a relative error of at most 0.0001.
Values sent between devices are 32-bit elements; how exact they have to be, the bound alone decides.
A program may use at most 128 MiB of HBM per device.

v0:
```python
import jax
import jax.numpy as jnp
from jax import lax
from jax.sharding import PartitionSpec as P


def spread(block, axis, owner):
    block = jnp.where(lax.axis_index(axis) == owner, block, jnp.zeros_like(block))
    return lax.psum(block, axis)


def gather_rows(normalized):
    return lax.all_gather(normalized, "col", axis=2, tiled=True)


def body(ancestor_inverse, panel, diag_inverse, structure, block_slot):
    highest = lax.Precision.HIGHEST
    row_count = lax.axis_size("row")
    col_count = lax.axis_size("col")
    row_index = lax.axis_index("row")
    col_index = lax.axis_index("col")
    node_count, slot_count, sub_rows, block_width = panel.shape
    total_slots = slot_count * row_count
    col_slots = total_slots // col_count
    slot_range = jnp.arange(total_slots, dtype=jnp.int32)
    lookup = (structure[:, :, None] == slot_range[None, None, :]).astype(jnp.int32)
    slot_ids = jnp.sum(lookup * block_slot[None, None, :], axis=2)
    chosen = jnp.any(slot_ids[:, :, None] == slot_range[None, None, :], axis=1).astype(jnp.int32)
    local_mask = lax.dynamic_slice_in_dim(chosen, row_index * slot_count, slot_count, 1)
    weight_mask = local_mask.astype(jnp.float32)[:, :, None, None]
    normalized = jnp.einsum("sqik,skw->sqiw", panel, diag_inverse, precision=highest) * weight_mask
    first_slot = col_index * col_slots
    owner_row = first_slot // slot_count
    row_panel = gather_rows(normalized)
    picked = lax.dynamic_slice_in_dim(row_panel, first_slot % slot_count, col_slots, 1)
    column_panel = spread(picked, "row", owner_row)
    column_rows = column_panel.reshape(node_count, col_slots * block_width, block_width)
    leading = jnp.einsum("sij,sik->sjk", diag_inverse, diag_inverse, precision=highest)
    partial_value = jnp.einsum("rc,scw->srw", ancestor_inverse, column_rows, precision=highest)
    partial_value = partial_value.reshape(node_count, slot_count, block_width, block_width)
    product = lax.psum_scatter(partial_value, "col", scatter_dimension=2, tiled=True) * weight_mask
    diag_terms = jnp.einsum("saiw,saiv->swv", normalized, product, precision=highest)
    diag_sum = lax.psum(diag_terms, ("row", "col"))
    return (-product, leading + diag_sum)


def solution(mesh):
    in_specs = (P("row", "col"), P(None, "row", "col", None), P(), P(), P())
    out_specs = (P(None, "row", "col", None), P())
    return jax.shard_map(body, mesh=mesh, in_specs=in_specs, out_specs=out_specs, check_vma=False)
```

profile of v0, /device:TPU:2, one launch (start us, length us, event | category | flops | bytes accessed | tf_op | source)
XLA Modules:
  0.0 785.4 jit_solution(1780212181948259479)
XLA Ops:
  7.2 0.0 copy-start
  7.2 0.0 all-gather.2.cloned.1.call-start
  7.2 1.1 select_reduce_fusion
  8.3 0.1 fusion.8
  8.4 0.1 dynamic-slice_convert_fusion
  8.5 0.1 copy-done
  8.6 2.8 fusion.3
  11.4 0.0 all-gather.2.cloned.1.call-update
  11.5 0.0 all-reduce.3.cloned.1.call-start
  11.5 132.8 %all-gather.2.cloned.1.call-done = f32[6,8,256,256]{3,2,1,0:T(8,128)} async-done(((f32[6,8,8,256]{3,2,1,0:T(8,128)}), f32[6,8,256,256]{3,2,1,0:T(8,128)}) %all-gather.2.cloned.1.call-update) | async-done | bytes 12582928 | tf_op jit(solution)/shard_map/all_gather | solution.py:13
  144.4 3.8 dynamic-slice_select_fusion
  148.2 3.5 copy.10
  151.7 0.0 all-reduce.3.cloned.1.call-update
  151.7 0.0 reduce-scatter.2.cloned.1.call-start
  151.8 143.7 %all-reduce.3.cloned.1.call-done = f32[6,512,256]{1,2,0:T(8,128)} async-done(((f32[6,512,256]{1,2,0:T(8,128)}), f32[6,512,256]{1,2,0:T(8,128)}) %all-reduce.3.cloned.1.call-update) | async-done | bytes 3145744 | tf_op jit(solution)/shard_map/psum | solution.py:9
  295.5 24.8 %convolution_bitcast_fusion = f32[6,2048,256]{1,2,0:T(8,128)} fusion(f32[6,512,256]{1,2,0:T(8,128)} %all-reduce.3.cloned.1.call-done, f32[2048,512]{1,0:T(8,128)} %param.5), kind=kOutput, calls=%fused_computation | convolution fusion | flops 19327352832 | bytes 19922944 | tf_op jit(solution)/shard_map/rc,scw->srw/dot_general | solution.py:39
  320.3 12.6 %copy.11 = f32[6,2048,256]{2,1,0:T(8,128)} copy(f32[6,2048,256]{1,2,0:T(8,128)} %convolution_bitcast_fusion) | data formatting | bytes 25165824 | tf_op jit(solution)/shard_map/rc,scw->srw/transpose | solution.py:39
  332.9 0.0 copy-start.1
  332.9 0.0 reduce-scatter.2.cloned.1.call-update
  332.9 0.2 all-reduce.5.cloned.1.call-start
  333.1 174.8 %reduce-scatter.2.cloned.1.call-done = f32[6,8,8,256]{3,2,1,0:T(8,128)} async-done(((f32[6,8,256,256]{3,2,1,0:T(8,128)}), f32[6,8,8,256]{3,2,1,0:T(8,128)}) %reduce-scatter.2.cloned.1.call-update) | async-done | bytes 393232 | tf_op jit(solution)/shard_map/reduce_scatter | solution.py:41
  507.9 0.0 copy-done.1
  507.9 0.0 copy-start.2
  507.9 3.8 convolution_bitcast_fusion.1
  511.7 0.0 all-reduce.5.cloned.1.call-update
  511.7 0.0 copy-done.2
  511.7 0.9 multiply_negate_fusion
  512.6 261.1 %all-reduce.5.cloned.1.call-done = f32[6,256,256]{2,1,0:T(8,128)} async-done(((f32[6,256,256]{2,1,0:T(8,128)}), f32[6,256,256]{2,1,0:T(8,128)}) %all-reduce.5.cloned.1.call-update) | async-done | bytes 1572880 | tf_op jit(solution)/shard_map/psum | solution.py:43
  773.7 5.2 convolution_add_fusion
  (1 shorter events, 0.0 us)
Async XLA Ops:
  7.2 1.4 copy-start
  7.2 137.2 %all-gather.2.cloned.1.call-start = ((), (), s32[]{:S(2)}) async-start(), calls=%async_computation.1 | async-start | bytes 12976128 | tf_op jit(solution)/shard_map/all_gather | solution.py:13
  11.5 284.0 %all-reduce.3.cloned.1.call-start = ((), (), s32[]{:S(2)}) async-start(), calls=%async_computation.2 | async-start | bytes 6291456 | tf_op jit(solution)/shard_map/psum | solution.py:9
  151.7 356.2 %reduce-scatter.2.cloned.1.call-start = ((), (), s32[]{:S(2)}) async-start(), calls=%async_computation.3 | async-start | bytes 12976128 | tf_op jit(solution)/shard_map/reduce_scatter | solution.py:41
  332.9 175.0 %copy-start.1 = (f32[6,8,8,256]{3,2,1,0:T(8,128)S(1)}, f32[6,8,8,256]{3,2,1,0:T(8,128)}, u32[]{:S(2)}) copy-start(f32[6,8,8,256]{3,2,1,0:T(8,128)} %fusion.3) | copy-start | bytes 1179652
  332.9 440.8 %all-reduce.5.cloned.1.call-start = ((), (), s32[]{:S(2)}) async-start(), calls=%async_computation.4 | async-start | bytes 3145728 | tf_op jit(solution)/shard_map/psum | solution.py:43
  507.9 3.8 copy-start.2
Sparse Core Ops, SparseCore 0:
  11.6 132.7 all-gather.1
  151.8 143.6 all-reduce.2
  333.0 174.8 reduce-scatter.1
  513.7 259.9 all-reduce.4
where the time goes:
time: 786 us; the launch traced here: 785 us
  waiting for transfers between devices  712 us (91%)
  matrix products  36.6 us (5%)
  local copies, waits for them, and re-layouts  16.3 us (2%)
  between operations  13.8 us (2%)
    psum x1, waiting for transfers between devices, body(): diag_sum = lax.psum(diag_terms, ('row', 'col'))  261 us
    reduce_scatter x1, waiting for transfers between devices, body(): lax.psum_scatter(partial_value, 'col', scatter_dimension=2, tiled=True)  175 us
    psum x1, waiting for transfers between devices, spread(): return lax.psum(block, axis)  144 us
    all_gather x1, waiting for transfers between devices, gather_rows(): return lax.all_gather(normalized, 'col', axis=2, tiled=True)  133 us
    dot_general x1, matrix products, body(): jnp.einsum('rc,scw->srw', ancestor_inverse, column_rows, precision=highest)  24.8 us
  transfers between devices with their start and end apart: 4, of which 4 were waited for; matrix products, arithmetic and copies ran while one was open for 0% of the time, Pallas kernels for 0%

commit v1 on v0

--- a/solution.py
+++ b/solution.py
@@ -40,7 +40,7 @@
     partial_value = partial_value.reshape(node_count, slot_count, block_width, block_width)
     product = lax.psum_scatter(partial_value, "col", scatter_dimension=2, tiled=True) * weight_mask
     diag_terms = jnp.einsum("saiw,saiv->swv", normalized, product, precision=highest)
-    diag_sum = lax.psum(diag_terms, ("row", "col"))
+    diag_sum = lax.psum(lax.psum(diag_terms, "row"), "col")
     return (-product, leading + diag_sum)
 
 

time: 786 us -> 893 us (1.14)
  waiting for transfers between devices: 712 us -> 818 us
    psum x1 -> x2, waiting for transfers between devices: 261 us -> 367 us  [body(): diag_sum = lax.psum(lax.psum(diag_terms, 'row'), 'col')]
  transfers between devices with their start and end apart: 4 -> 5, of which waited for: 4 -> 5; matrix products, arithmetic and copies ran while one was open for 0% -> 0% of each run, Pallas kernels for 0% -> 0%
where the time goes in v1:
time: 893 us; the launch traced here: 891 us
  waiting for transfers between devices  818 us (92%)
  matrix products  36.7 us (4%)
  local copies, waits for them, and re-layouts  16.3 us (2%)
  between operations  13.8 us (2%)
    psum x2, waiting for transfers between devices, body(): diag_sum = lax.psum(lax.psum(diag_terms, 'row'), 'col')  367 us
    reduce_scatter x1, waiting for transfers between devices, body(): lax.psum_scatter(partial_value, 'col', scatter_dimension=2, tiled=True)  175 us
    psum x1, waiting for transfers between devices, spread(): return lax.psum(block, axis)  144 us
    all_gather x1, waiting for transfers between devices, gather_rows(): return lax.all_gather(normalized, 'col', axis=2, tiled=True)  133 us
    dot_general x1, matrix products, body(): jnp.einsum('rc,scw->srw', ancestor_inverse, column_rows, precision=highest)  24.8 us
  transfers between devices with their start and end apart: 5, of which 5 were waited for; matrix products, arithmetic and copies ran while one was open for 0% of the time, Pallas kernels for 0%

profile of v1, /device:TPU:2, one launch (start us, length us, event | category | flops | bytes accessed | tf_op | source)
XLA Modules:
  0.0 891.2 jit_solution(17210796001445058578)
XLA Ops:
  7.2 0.0 copy-start
  7.2 0.0 all-gather.2.cloned.1.call-start
  7.2 1.1 select_reduce_fusion
  8.3 0.1 fusion.8
  8.4 0.1 dynamic-slice_convert_fusion
  8.5 0.1 copy-done
  8.6 2.8 fusion.3
  11.4 0.0 all-gather.2.cloned.1.call-update
  11.5 0.0 all-reduce.4.cloned.1.call-start
  11.5 132.8 %all-gather.2.cloned.1.call-done = f32[6,8,256,256]{3,2,1,0:T(8,128)} async-done(((f32[6,8,8,256]{3,2,1,0:T(8,128)}), f32[6,8,256,256]{3,2,1,0:T(8,128)}) %all-gather.2.cloned.1.call-update) | async-done | bytes 12582928 | tf_op jit(solution)/shard_map/all_gather | solution.py:13
  144.4 3.8 dynamic-slice_select_fusion
  148.2 3.5 copy.10
  151.7 0.0 all-reduce.4.cloned.1.call-update
  151.7 0.0 reduce-scatter.2.cloned.1.call-start
  151.8 143.7 %all-reduce.4.cloned.1.call-done = f32[6,512,256]{1,2,0:T(8,128)} async-done(((f32[6,512,256]{1,2,0:T(8,128)}), f32[6,512,256]{1,2,0:T(8,128)}) %all-reduce.4.cloned.1.call-update) | async-done | bytes 3145744 | tf_op jit(solution)/shard_map/psum | solution.py:9
  295.5 24.8 %convolution_bitcast_fusion = f32[6,2048,256]{1,2,0:T(8,128)} fusion(f32[6,512,256]{1,2,0:T(8,128)} %all-reduce.4.cloned.1.call-done, f32[2048,512]{1,0:T(8,128)} %param.5), kind=kOutput, calls=%fused_computation | convolution fusion | flops 19327352832 | bytes 19922944 | tf_op jit(solution)/shard_map/rc,scw->srw/dot_general | solution.py:39
  320.3 12.6 %copy.11 = f32[6,2048,256]{2,1,0:T(8,128)} copy(f32[6,2048,256]{1,2,0:T(8,128)} %convolution_bitcast_fusion) | data formatting | bytes 25165824 | tf_op jit(solution)/shard_map/rc,scw->srw/transpose | solution.py:39
  332.9 0.0 copy-start.1
  332.9 0.0 reduce-scatter.2.cloned.1.call-update
  332.9 0.0 all-reduce.6.cloned.1.call-start
  332.9 174.9 %reduce-scatter.2.cloned.1.call-done = f32[6,8,8,256]{3,2,1,0:T(8,128)} async-done(((f32[6,8,256,256]{3,2,1,0:T(8,128)}), f32[6,8,8,256]{3,2,1,0:T(8,128)}) %reduce-scatter.2.cloned.1.call-update) | async-done | bytes 393232 | tf_op jit(solution)/shard_map/reduce_scatter | solution.py:41
  507.9 0.0 copy-done.1
  507.9 0.0 copy-start.2
  507.9 3.8 convolution_bitcast_fusion.1
  511.7 0.0 all-reduce.6.cloned.1.call-update
  511.7 0.2 all-reduce.8.cloned.1.call-start
  512.0 90.8 %all-reduce.6.cloned.1.call-done = f32[6,256,256]{2,1,0:T(8,128)} async-done(((f32[6,256,256]{2,1,0:T(8,128)}), f32[6,256,256]{2,1,0:T(8,128)}) %all-reduce.6.cloned.1.call-update) | async-done | bytes 1572880 | tf_op jit(solution)/shard_map/psum | solution.py:43
  602.8 0.0 all-reduce.8.cloned.1.call-update
  602.8 0.0 copy-done.2
  602.8 0.9 multiply_negate_fusion
  603.7 275.8 %all-reduce.8.cloned.1.call-done = f32[6,256,256]{2,1,0:T(8,128)} async-done(((f32[6,256,256]{2,1,0:T(8,128)}), f32[6,256,256]{2,1,0:T(8,128)}) %all-reduce.8.cloned.1.call-update) | async-done | bytes 1572880 | tf_op jit(solution)/shard_map/psum | solution.py:43
  879.4 5.2 convolution_add_fusion
  (1 shorter events, 0.0 us)
Async XLA Ops:
  7.2 1.4 copy-start
  7.2 137.2 %all-gather.2.cloned.1.call-start = ((), (), s32[]{:S(2)}) async-start(), calls=%async_computation.1 | async-start | bytes 12976128 | tf_op jit(solution)/shard_map/all_gather | solution.py:13
  11.5 284.0 %all-reduce.4.cloned.1.call-start = ((), (), s32[]{:S(2)}) async-start(), calls=%async_computation.2 | async-start | bytes 6291456 | tf_op jit(solution)/shard_map/psum | solution.py:9
  151.7 356.2 %reduce-scatter.2.cloned.1.call-start = ((), (), s32[]{:S(2)}) async-start(), calls=%async_computation.3 | async-start | bytes 12976128 | tf_op jit(solution)/shard_map/reduce_scatter | solution.py:41
  332.9 175.0 %copy-start.1 = (f32[6,8,8,256]{3,2,1,0:T(8,128)S(1)}, f32[6,8,8,256]{3,2,1,0:T(8,128)}, u32[]{:S(2)}) copy-start(f32[6,8,8,256]{3,2,1,0:T(8,128)} %fusion.3) | copy-start | bytes 1179652
  332.9 269.9 %all-reduce.6.cloned.1.call-start = ((), (), s32[]{:S(2)}) async-start(), calls=%async_computation.4 | async-start | bytes 3145728 | tf_op jit(solution)/shard_map/psum | solution.py:43
  507.9 94.9 %copy-start.2 = (f32[6,8,8,256]{3,2,1,0:T(8,128)S(1)}, f32[6,8,8,256]{3,2,1,0:T(8,128)}, u32[]{:S(2)}) copy-start(f32[6,8,8,256]{3,2,1,0:T(8,128)} %reduce-scatter.2.cloned.1.call-done) | copy-start | bytes 1179652
  511.7 367.7 %all-reduce.8.cloned.1.call-start = ((), (), s32[]{:S(2)}) async-start(), calls=%async_computation.5 | async-start | bytes 3145728 | tf_op jit(solution)/shard_map/psum | solution.py:43
Sparse Core Ops, SparseCore 0:
  11.6 132.7 all-gather.1
  151.8 143.6 all-reduce.3
  333.0 174.8 reduce-scatter.1
  511.8 90.8 all-reduce.5
  605.2 274.1 all-reduce.7
